TPU v7x, 256 devices: a whole 4x4x8 slice. The times are simulated.
256 devices in a mesh: table: 16 (over x, y), dp: 8 (over z), col: 2 (over core).
Axes of the slice: x: 4, y: 4, z: 8, core: 2. Of those that a mesh axis runs over, the one named last changes fastest.
Arguments:
- table_weights: float32 [32768, 512], P('table', 'col'), may hold values from -6 to 6
- moment_first: float32 [32768, 512], P('table', 'col'), may hold values from -3 to 3
- moment_second: float32 [32768], P('table'), may hold values from 0.1 to 2
- hot_slices: int32 [16, 2], replicated, may hold values from 0 to 31, as said below
- upstream_grad: bfloat16 [131072, 512], P(('table', 'dp'), 'col'), may hold values from -20 to 20
- dedup_map: int32 [131072, 32], P(('table', 'dp')), may hold values from 0 to 4095, as said below
- unique_rows: int32 [128, 16, 256], P(('table', 'dp')), may hold values from 0 to 32767, as said below
- row_counts: int32 [128, 16], P(('table', 'dp')), may hold values from 192 to 256, as said below
Outputs:
- new_weights: float32 [32768, 512], P('table', 'col')
- new_first: float32 [32768, 512], P('table', 'col')
- new_second: float32 [32768], P('table')
Inputs may be any that keep to these rules, and one draw needn't show every extreme that they name: `hot_slices`: each row holds 2 different slice numbers below 32. `unique_rows`: for source device s and owner t, the first row_counts[s, t] entries are different rows r with physical(r) on table index t; the remaining entries are not used. `row_counts`: in every draw some owner receives 256 used slots from every source device. `dedup_map`: an entry in a row of source device s is a used slot t * 256 + k with k < row_counts[s, t].
All inputs are finite; a program needn't handle non-finite values.
Results may differ from a plain program's by a relative error of at most 0.0003.
Values sent between devices are 32-bit elements; how exact they have to be, the bound alone decides.
No kernel may reach another device: no remote copies, remote signals or barrier semaphores. Data moves between devices by JAX's collectives and lax.ppermute only.
A program may use at most 64 MiB of HBM per device.

v0:
```python
import jax
import jax.numpy as jnp
from jax import lax
from jax.sharding import PartitionSpec as P

SLICE = 64
beta_one = 0.9
beta_two = 0.99
learn_rate = 0.1
eps_value = 1e-08


def partner_2(block, axis, distance):
    count = lax.axis_size(axis)
    route = []
    for low in range(count):
        high = low | 1 << distance
        if high != low and high < count:
            route += [(low, high), (high, low)]
    return lax.ppermute(block, axis, route)


def local_targets(logical_rows, hot_slices, rows_dev):
    n_table = hot_slices.shape[0]
    row_owner = logical_rows // rows_dev
    local_row = logical_rows % rows_dev
    row_piece = local_row // SLICE
    row_offset = local_row % SLICE
    matches = hot_slices[row_owner] == row_piece[..., None]
    partner = (row_owner + n_table // 2) % n_table
    partner_piece = jnp.sum(jnp.where(matches, hot_slices[partner], 0), axis=-1)
    return jnp.where(jnp.any(matches, axis=-1), partner_piece * SLICE + row_offset, local_row)


def adam_rows(weights, first, second, gradient, squares, full_width):
    new_second = beta_two * second + (1.0 - beta_two) * (squares / full_width)
    new_first = beta_one * first + (1.0 - beta_one) * gradient
    scaled = jnp.sqrt(new_second / (1.0 - beta_two**8)) + eps_value
    new_weights = weights - learn_rate * (new_first / (1.0 - beta_one**8)) / scaled[:, None]
    return (new_weights, new_first, new_second)


def on_device(
    table_weights,
    moment_first,
    moment_second,
    hot_slices,
    upstream_grad,
    dedup_map,
    unique_rows,
    row_counts,
):
    n_table = lax.axis_size("table")
    position = lax.axis_index("table")
    rows_dev, col_width = table_weights.shape
    own_hot = hot_slices[position]
    n_hots = own_hot.shape[0]
    starts = [own_hot[k] * SLICE for k in range(n_hots)]
    out_weights = jnp.stack(
        [lax.dynamic_slice_in_dim(table_weights, starts[k], SLICE, 0) for k in range(n_hots)]
    )
    out_first = jnp.stack(
        [lax.dynamic_slice_in_dim(moment_first, starts[k], SLICE, 0) for k in range(n_hots)]
    )
    out_second = jnp.stack(
        [lax.dynamic_slice_in_dim(moment_second, starts[k], SLICE, 0) for k in range(n_hots)]
    )
    swap_bit = n_table.bit_length() - 2
    incoming = partner_2((out_weights, out_first, out_second), "table", swap_bit)
    placed_weights = table_weights
    placed_first = moment_first
    placed_second = moment_second
    for k in range(n_hots):
        placed_weights = lax.dynamic_update_slice_in_dim(
            placed_weights, incoming[0][k], starts[k], 0
        )
        placed_first = lax.dynamic_update_slice_in_dim(placed_first, incoming[1][k], starts[k], 0)
        placed_second = lax.dynamic_update_slice_in_dim(placed_second, incoming[2][k], starts[k], 0)
    slot_cap = unique_rows.shape[2]
    valid = jnp.arange(slot_cap)[None, :] < row_counts[0][:, None]
    targets = jnp.where(valid, local_targets(unique_rows[0], hot_slices, rows_dev), rows_dev)
    slot_iota = jnp.arange(slot_cap)

    def owner_block(carry, owner):
        wanted = slot_iota + owner * slot_cap
        tally = jnp.sum(
            (dedup_map[None, :, :] == wanted[:, None, None]).astype(jnp.float32), axis=2
        )
        block = jnp.dot(
            tally.astype(jnp.bfloat16), upstream_grad, preferred_element_type=jnp.float32
        )
        return (carry, block)

    _, slot_grad = lax.scan(owner_block, 0, jnp.arange(n_table))
    got_grad, got_target = (
        lax.all_to_all(slot_grad, "table", split_axis=0, concat_axis=0, tiled=True),
        lax.all_to_all(targets, "table", split_axis=0, concat_axis=0, tiled=True),
    )
    row_iota = jnp.arange(rows_dev)

    def add_source(total, inputs):
        grad_block, target_block = inputs
        select = (row_iota[:, None] == target_block[None, :]).astype(jnp.float32)
        return (
            total
            + jnp.dot(
                select,
                grad_block,
                precision=lax.Precision.HIGHEST,
                preferred_element_type=jnp.float32,
            ),
            None,
        )

    dense, _ = lax.scan(
        add_source, jnp.zeros((rows_dev, col_width), jnp.float32), (got_grad, got_target)
    )
    full_width = col_width * lax.axis_size("col")
    gradient = lax.psum(dense, "dp")
    squares = lax.psum(jnp.sum(gradient * gradient, axis=1), "col")
    new_weights, new_first, new_second = adam_rows(
        placed_weights, placed_first, placed_second, gradient, squares, full_width
    )
    return (new_weights, new_first, new_second)


def solution(mesh):
    placed = (
        P("table", "col"),
        P("table", "col"),
        P("table"),
        P(),
        P(("table", "dp"), "col"),
        P(("table", "dp"), None),
        P(("table", "dp"), None, None),
        P(("table", "dp"), None),
    )
    return jax.shard_map(
        on_device,
        mesh=mesh,
        in_specs=placed,
        out_specs=(P("table", "col"), P("table", "col"), P("table")),
        check_vma=False,
    )
```

profile of v0, /device:TPU:1, one launch (start us, length us, event | category | flops | bytes accessed | tf_op | source)
XLA Modules:
  0.0 479.1 jit_solution(15004162492710192044)
XLA Ops:
  7.2 3.2 copy.52
  10.4 1.3 copy.53
  11.9 10.8 %gather_fusion = s32[4096,2]{1,0:T(8,128)S(1)} fusion(s32[16,2]{1,0:T(8,128)S(1)} %copy.21, s32[4096]{0:T(1024)S(1)} %broadcast_clamp_fusion.1), kind=kCustom, calls=%fused_computation | custom fusion | bytes 81920 | tf_op jit(solution)/shard_map/gather | solution.py:29
  22.7 14.1 %gather_fusion.1 = s32[4096,2]{1,0:T(8,128)} fusion(s32[16,2]{1,0:T(8,128)S(1)} %copy.21, s32[4096]{0:T(1024)S(1)} %broadcast_clamp_fusion), kind=kCustom, calls=%fused_computation.1 | custom fusion | bytes 81920 | tf_op jit(solution)/shard_map/gather | solution.py:31
  36.8 1.3 fusion.29
  39.8 7.6 %all-to-all-start = ((s32[16,1,256]{2,1,0:T(1,128)}), s32[16,1,256]{2,1,0:T(1,128)S(1)}, u32[]{:S(2)}, u32[]{:S(2)}) async-start(s32[16,1,256]{2,1,0:T(1,128)} %copy.23), calls=%async_computation | async-start | bytes 32768 | tf_op jit(solution)/shard_map/all_to_all | solution.py:97
  47.4 217.9 %while.22 = (s32[]{:T(128)}, f32[16,256,256]{2,1,0:T(8,128)}, s32[1024,32]{0,1:T(8,128)S(1)}, s32[16]{0:T(128)S(1)}, bf16[1024,256]{1,0:T(8,128)(2,1)S(1)}, /*index=5*/s32[]{:T(128)}, s32[1]{0:T(128)}) while((s32[]{:T(128)}, f32[16,256,256]{2,1,0:T(8,128)}, s32[1024,32]{0,1:T(8,128)S(1)}, s32[16]{0:T(128)S(1)}, ...), condition=%wide.region_2.3_spmd.clone, body=%wide.region_0.2_spmd.clone.sunk | while | flops 159121664 | bytes 1968745 | solution.py:94
  48.9 11.3 %convert_reduce_fusion.2 = bf16[256,1024]{1,0:T(8,128)(2,1)S(1)} fusion(s32[1024,32]{0,1:T(8,128)S(1)} %get-tuple-element.201, s32[256]{0:T(256)S(1)} %iota_add_fusion.2), kind=kLoop, calls=%fused_computation.4.clone.1 | loop fusion | flops 24903680 | bytes 656384 | tf_op jit(solution)/shard_map/while/body/eval_jaxpr/reduce_sum | solution.py:86
  60.2 1.0 fusion.39
  62.5 11.3 %convert_reduce_fusion.2 = bf16[256,1024]{1,0:T(8,128)(2,1)S(1)} fusion(s32[1024,32]{0,1:T(8,128)S(1)} %get-tuple-element.201, s32[256]{0:T(256)S(1)} %iota_add_fusion.2), kind=kLoop, calls=%fused_computation.4.clone.1 | loop fusion | flops 24903680 | bytes 656384 | tf_op jit(solution)/shard_map/while/body/eval_jaxpr/reduce_sum | solution.py:86
  73.8 1.0 fusion.39
  76.1 11.3 %convert_reduce_fusion.2 = bf16[256,1024]{1,0:T(8,128)(2,1)S(1)} fusion(s32[1024,32]{0,1:T(8,128)S(1)} %get-tuple-element.201, s32[256]{0:T(256)S(1)} %iota_add_fusion.2), kind=kLoop, calls=%fused_computation.4.clone.1 | loop fusion | flops 24903680 | bytes 656384 | tf_op jit(solution)/shard_map/while/body/eval_jaxpr/reduce_sum | solution.py:86
  87.4 1.0 fusion.39
  89.7 11.3 %convert_reduce_fusion.2 = bf16[256,1024]{1,0:T(8,128)(2,1)S(1)} fusion(s32[1024,32]{0,1:T(8,128)S(1)} %get-tuple-element.201, s32[256]{0:T(256)S(1)} %iota_add_fusion.2), kind=kLoop, calls=%fused_computation.4.clone.1 | loop fusion | flops 24903680 | bytes 656384 | tf_op jit(solution)/shard_map/while/body/eval_jaxpr/reduce_sum | solution.py:86
  101.0 1.0 fusion.39
  103.3 11.3 %convert_reduce_fusion.2 = bf16[256,1024]{1,0:T(8,128)(2,1)S(1)} fusion(s32[1024,32]{0,1:T(8,128)S(1)} %get-tuple-element.201, s32[256]{0:T(256)S(1)} %iota_add_fusion.2), kind=kLoop, calls=%fused_computation.4.clone.1 | loop fusion | flops 24903680 | bytes 656384 | tf_op jit(solution)/shard_map/while/body/eval_jaxpr/reduce_sum | solution.py:86
  114.6 1.0 fusion.39
  116.9 11.3 %convert_reduce_fusion.2 = bf16[256,1024]{1,0:T(8,128)(2,1)S(1)} fusion(s32[1024,32]{0,1:T(8,128)S(1)} %get-tuple-element.201, s32[256]{0:T(256)S(1)} %iota_add_fusion.2), kind=kLoop, calls=%fused_computation.4.clone.1 | loop fusion | flops 24903680 | bytes 656384 | tf_op jit(solution)/shard_map/while/body/eval_jaxpr/reduce_sum | solution.py:86
  128.2 1.0 fusion.39
  130.5 11.3 %convert_reduce_fusion.2 = bf16[256,1024]{1,0:T(8,128)(2,1)S(1)} fusion(s32[1024,32]{0,1:T(8,128)S(1)} %get-tuple-element.201, s32[256]{0:T(256)S(1)} %iota_add_fusion.2), kind=kLoop, calls=%fused_computation.4.clone.1 | loop fusion | flops 24903680 | bytes 656384 | tf_op jit(solution)/shard_map/while/body/eval_jaxpr/reduce_sum | solution.py:86
  141.8 1.0 fusion.39
  144.1 11.3 %convert_reduce_fusion.2 = bf16[256,1024]{1,0:T(8,128)(2,1)S(1)} fusion(s32[1024,32]{0,1:T(8,128)S(1)} %get-tuple-element.201, s32[256]{0:T(256)S(1)} %iota_add_fusion.2), kind=kLoop, calls=%fused_computation.4.clone.1 | loop fusion | flops 24903680 | bytes 656384 | tf_op jit(solution)/shard_map/while/body/eval_jaxpr/reduce_sum | solution.py:86
  157.7 11.3 %convert_reduce_fusion.2 = bf16[256,1024]{1,0:T(8,128)(2,1)S(1)} fusion(s32[1024,32]{0,1:T(8,128)S(1)} %get-tuple-element.201, s32[256]{0:T(256)S(1)} %iota_add_fusion.2), kind=kLoop, calls=%fused_computation.4.clone.1 | loop fusion | flops 24903680 | bytes 656384 | tf_op jit(solution)/shard_map/while/body/eval_jaxpr/reduce_sum | solution.py:86
  169.0 1.0 fusion.39
  171.3 11.3 %convert_reduce_fusion.2 = bf16[256,1024]{1,0:T(8,128)(2,1)S(1)} fusion(s32[1024,32]{0,1:T(8,128)S(1)} %get-tuple-element.201, s32[256]{0:T(256)S(1)} %iota_add_fusion.2), kind=kLoop, calls=%fused_computation.4.clone.1 | loop fusion | flops 24903680 | bytes 656384 | tf_op jit(solution)/shard_map/while/body/eval_jaxpr/reduce_sum | solution.py:86
  182.6 1.0 fusion.39
  184.9 11.3 %convert_reduce_fusion.2 = bf16[256,1024]{1,0:T(8,128)(2,1)S(1)} fusion(s32[1024,32]{0,1:T(8,128)S(1)} %get-tuple-element.201, s32[256]{0:T(256)S(1)} %iota_add_fusion.2), kind=kLoop, calls=%fused_computation.4.clone.1 | loop fusion | flops 24903680 | bytes 656384 | tf_op jit(solution)/shard_map/while/body/eval_jaxpr/reduce_sum | solution.py:86
  196.2 1.0 fusion.39
  198.5 11.3 %convert_reduce_fusion.2 = bf16[256,1024]{1,0:T(8,128)(2,1)S(1)} fusion(s32[1024,32]{0,1:T(8,128)S(1)} %get-tuple-element.201, s32[256]{0:T(256)S(1)} %iota_add_fusion.2), kind=kLoop, calls=%fused_computation.4.clone.1 | loop fusion | flops 24903680 | bytes 656384 | tf_op jit(solution)/shard_map/while/body/eval_jaxpr/reduce_sum | solution.py:86
  209.8 1.0 fusion.39
  212.1 11.3 %convert_reduce_fusion.2 = bf16[256,1024]{1,0:T(8,128)(2,1)S(1)} fusion(s32[1024,32]{0,1:T(8,128)S(1)} %get-tuple-element.201, s32[256]{0:T(256)S(1)} %iota_add_fusion.2), kind=kLoop, calls=%fused_computation.4.clone.1 | loop fusion | flops 24903680 | bytes 656384 | tf_op jit(solution)/shard_map/while/body/eval_jaxpr/reduce_sum | solution.py:86
  225.7 11.3 %convert_reduce_fusion.2 = bf16[256,1024]{1,0:T(8,128)(2,1)S(1)} fusion(s32[1024,32]{0,1:T(8,128)S(1)} %get-tuple-element.201, s32[256]{0:T(256)S(1)} %iota_add_fusion.2), kind=kLoop, calls=%fused_computation.4.clone.1 | loop fusion | flops 24903680 | bytes 656384 | tf_op jit(solution)/shard_map/while/body/eval_jaxpr/reduce_sum | solution.py:86
  237.1 1.0 fusion.39
  239.3 11.3 %convert_reduce_fusion.2 = bf16[256,1024]{1,0:T(8,128)(2,1)S(1)} fusion(s32[1024,32]{0,1:T(8,128)S(1)} %get-tuple-element.201, s32[256]{0:T(256)S(1)} %iota_add_fusion.2), kind=kLoop, calls=%fused_computation.4.clone.1 | loop fusion | flops 24903680 | bytes 656384 | tf_op jit(solution)/shard_map/while/body/eval_jaxpr/reduce_sum | solution.py:86
  252.9 11.3 %convert_reduce_fusion.2 = bf16[256,1024]{1,0:T(8,128)(2,1)S(1)} fusion(s32[1024,32]{0,1:T(8,128)S(1)} %get-tuple-element.201, s32[256]{0:T(256)S(1)} %iota_add_fusion.2), kind=kLoop, calls=%fused_computation.4.clone.1 | loop fusion | flops 24903680 | bytes 656384 | tf_op jit(solution)/shard_map/while/body/eval_jaxpr/reduce_sum | solution.py:86
  264.2 1.0 fusion.39
  265.3 6.7 %all-to-all-start.1 = ((f32[16,256,256]{2,1,0:T(8,128)}), f32[16,256,256]{2,1,0:T(8,128)}, u32[]{:S(2)}, u32[]{:S(2)}) async-start(f32[16,256,256]{2,1,0:T(8,128)} %get-tuple-element.62), calls=%async_computation.1 | async-start | bytes 8388608 | tf_op jit(solution)/shard_map/all_to_all | solution.py:96
  272.1 51.8 %all-to-all-done.1 = f32[16,256,256]{2,1,0:T(8,128)} async-done(((f32[16,256,256]{2,1,0:T(8,128)}), f32[16,256,256]{2,1,0:T(8,128)}, u32[]{:S(2)}, u32[]{:S(2)}) %all-to-all-start.1) | async-done | bytes 4194336 | tf_op jit(solution)/shard_map/all_to_all | solution.py:96
  323.9 45.4 %while.23 = (s32[]{:T(128)}, f32[2048,256]{1,0:T(8,128)S(1)}, s32[16,256]{1,0:T(8,128)S(1)}, f32[16,256,256]{2,1,0:T(8,128)}, s32[]{:T(128)}, /*index=5*/s32[]{:T(128)}) while((s32[]{:T(128)}, f32[2048,256]{1,0:T(8,128)S(1)}, s32[16,256]{1,0:T(8,128)S(1)}, f32[16,256,256]{2,1,0:T(8,128)}, s32[]{:T(128)}, /*index=5*/s32[]{:T(128)}) %tuple.62), condition=%wide.region_6.7_spmd.clone, body=%wide.region_5.6_spmd.clone.sunk | while | flops 1612185600 | bytes 4460115 | solution.py:115
  323.9 2.8 convolution_add_fusion.2
  326.7 2.8 convolution_add_fusion.2
  329.6 2.8 convolution_add_fusion.2
  332.4 2.8 convolution_add_fusion.2
  335.2 2.8 convolution_add_fusion.2
  338.1 2.8 convolution_add_fusion.2
  340.9 2.8 convolution_add_fusion.2
  343.8 2.8 convolution_add_fusion.2
  346.6 2.8 convolution_add_fusion.2
  349.4 2.8 convolution_add_fusion.2
  352.3 2.8 convolution_add_fusion.2
  355.1 2.8 convolution_add_fusion.2
  358.0 2.8 convolution_add_fusion.2
  360.8 2.8 convolution_add_fusion.2
  363.6 2.8 convolution_add_fusion.2
  366.5 2.8 convolution_add_fusion.2
  369.3 1.3 copy-done
  373.5 4.6 collective-permute-start.1
  378.2 3.0 collective-permute-start
  381.3 1.2 collective-permute-done.2
  383.9 1.0 collective-permute-done
  386.2 73.0 %all-reduce.2.cloned.1.call-done = f32[2048,256]{1,0:T(8,128)} async-done(((f32[2048,256]{1,0:T(8,128)}), f32[2048,256]{1,0:T(8,128)}) %all-reduce.2.cloned.1.call-update) | async-done | bytes 2097168 | tf_op jit(solution)/shard_map/psum | solution.py:119
  459.1 1.9 multiply_reduce_fusion
  461.1 5.8 %psum.15 = f32[2048]{0:T(1024)S(1)} all-reduce(f32[2048]{0:T(1024)S(1)} %multiply_reduce_fusion), channel_id=1, replica_groups=mesh['table'=16,'dp'=8,'col'=2] {'col'}, use_global_device_ids=true, to_apply=%region_9.10 | all-reduce | flops 2048 | bytes 16384 | tf_op jit(solution)/shard_map/psum | solution.py:120
  467.5 4.8 divide_subtract_fusion
  (104 shorter events, 19.9 us)
Async XLA Ops:
  7.2 3.2 copy-start.5
  10.4 1.3 copy-start.7
  10.4 1.3 copy-start.6
  10.4 1.4 copy-start.8
  36.8 1.6 copy-start.3
  36.8 2.3 copy-start.9
  36.8 10.6 %copy-start.1 = (bf16[1024,256]{1,0:T(8,128)(2,1)S(1)}, bf16[1024,256]{1,0:T(8,128)(2,1)}, u32[]{:S(2)}) copy-start(bf16[1024,256]{1,0:T(8,128)(2,1)} %param.16) | copy-start | bytes 1572868
  36.8 10.6 %copy-start.4 = (s32[1024,32]{0,1:T(8,128)S(1)}, s32[1024,32]{0,1:T(8,128)}, u32[]{:S(2)}) copy-start(s32[1024,32]{0,1:T(8,128)} %param.17) | copy-start | bytes 393220
  39.8 225.5 %all-to-all-start = ((s32[16,1,256]{2,1,0:T(1,128)}), s32[16,1,256]{2,1,0:T(1,128)S(1)}, u32[]{:S(2)}, u32[]{:S(2)}) async-start(s32[16,1,256]{2,1,0:T(1,128)} %copy.23), calls=%async_computation | async-start | bytes 32768 | tf_op jit(solution)/shard_map/all_to_all | solution.py:97
  265.3 58.6 %all-to-all-start.1 = ((f32[16,256,256]{2,1,0:T(8,128)}), f32[16,256,256]{2,1,0:T(8,128)}, u32[]{:S(2)}, u32[]{:S(2)}) async-start(f32[16,256,256]{2,1,0:T(8,128)} %get-tuple-element.62), calls=%async_computation.1 | async-start | bytes 8388608 | tf_op jit(solution)/shard_map/all_to_all | solution.py:96
  272.0 187.1 %all-reduce.2.cloned.1.call-start = ((), (), s32[]{:S(2)}) async-start(), calls=%async_computation.2 | async-start | bytes 4194304 | tf_op jit(solution)/shard_map/psum | solution.py:119
  369.3 1.3 copy-start
  373.5 9.1 %collective-permute-start.1 = (f32[2,64,256]{2,1,0:T(8,128)S(1)}, f32[2,64,256]{2,1,0:T(8,128)S(1)}, u32[]{:S(2)}, u32[]{:S(2)}) collective-permute-start(f32[2,64,256]{2,1,0:T(8,128)S(1)} %pad_maximum_fusion.1), channel_id=1, source_target_pairs={{0,128},{128,0},{16,144},{144,16},{32,160},{160,32},{48,176},{176,... | collective-permute-start | bytes 393224 | tf_op jit(solution)/shard_map/ppermute | solution.py:20
  378.1 4.3 collective-permute-start.2
  378.2 6.7 %collective-permute-start = (f32[2,64,256]{2,1,0:T(8,128)S(1)}, f32[2,64,256]{2,1,0:T(8,128)S(1)}, u32[]{:S(2)}, u32[]{:S(2)}) collective-permute-start(f32[2,64,256]{2,1,0:T(8,128)S(1)} %pad_maximum_fusion), channel_id=1, source_target_pairs={{0,128},{128,0},{16,144},{144,16},{32,160},{160,32},{48,176},{176,... | collective-permute-start | bytes 393224 | tf_op jit(solution)/shard_map/ppermute | solution.py:20
  386.2 81.4 %copy-start.2 = (f32[2048,256]{1,0:T(8,128)S(1)}, f32[2048,256]{1,0:T(8,128)}, u32[]{:S(2)}) copy-start(f32[2048,256]{1,0:T(8,128)} %fusion.12) | copy-start | bytes 6291460
Sparse Core Ops, SparseCore 0:
  370.8 88.3 all-reduce.1
where the time goes:
time: 480 us; the launch traced here: 479 us
  other arithmetic  191 us (40%)
  waiting for transfers between devices  127 us (26%)
  matrix products  60.9 us (13%)
  local copies, waits for them, and re-layouts  45.9 us (10%)
  starting transfers between devices  22 us (5%)
  between operations  15.5 us (3%)
  loops' own time  11.2 us (2%)
  blocking collectives  5.83 us (1%)
    reduce_sum x16, other arithmetic, owner_block(): jnp.sum((dedup_map[None, :, :] == wanted[:, None, None]).astype(jnp.float...  181 us
    psum x1, waiting for transfers between devices, on_device(): gradient = lax.psum(dense, 'dp')  73 us
    all_to_all x1, waiting for transfers between devices, on_device(): lax.all_to_all(slot_grad, 'table', split_axis=0, concat_axis=0, tiled=True)  51.8 us
    dot_general x16, matrix products, add_source(): jnp.dot(select, grad_block, precision=lax.Precision.HIGHEST, preferred_el...  44.7 us
    dot_general x16, matrix products, owner_block(): jnp.dot(tally.astype(jnp.bfloat16), upstream_grad, preferred_element_type...  16.2 us
    gather x1, local copies, waits for them, and re-layouts, local_targets(): partner_piece = jnp.sum(jnp.where(matches, hot_slices[partner], 0), axis=-1)  14.1 us
    gather x1, local copies, waits for them, and re-layouts, local_targets(): matches = hot_slices[row_owner] == row_piece[..., None]  10.8 us
    another operation x1, loops' own time, on_device(): _, slot_grad = lax.scan(owner_block, 0, jnp.arange(n_table))  10.7 us
  transfers between devices with their start and end apart: 6, of which 4 were waited for; matrix products, arithmetic and copies ran while one was open for 44% of the time, Pallas kernels for 0%

commit v1 on v0

--- a/solution.py
+++ b/solution.py
@@ -116,7 +116,7 @@
         add_source, jnp.zeros((rows_dev, col_width), jnp.float32), (got_grad, got_target)
     )
     full_width = col_width * lax.axis_size("col")
-    gradient = lax.psum(dense, "dp")
+    gradient = jnp.sum(lax.all_gather(dense, "dp"), axis=0)
     squares = lax.psum(jnp.sum(gradient * gradient, axis=1), "col")
     new_weights, new_first, new_second = adam_rows(
         placed_weights, placed_first, placed_second, gradient, squares, full_width

time: 480 us -> 577 us (1.20)
  waiting for transfers between devices: 127 us -> 221 us
    all_gather x0 -> x1, waiting for transfers between devices: none -> 166 us  [on_device(): gradient = jnp.sum(lax.all_gather(dense, 'dp'), axis=0)]
    psum x1 -> x0, waiting for transfers between devices: 73 us -> none  [on_device(): gradient = lax.psum(dense, 'dp')]
    reduce_sum x0 -> x1, other arithmetic: none -> 7.14 us  [on_device(): gradient = jnp.sum(lax.all_gather(dense, 'dp'), axis=0)]
  transfers between devices with their start and end apart: 6 -> 6, of which waited for: 4 -> 4; matrix products, arithmetic and copies ran while one was open for 44% -> 37% of each run, Pallas kernels for 0% -> 0%
where the time goes in v1:
time: 577 us; the launch traced here: 576 us
  waiting for transfers between devices  221 us (38%)
  other arithmetic  196 us (34%)
  matrix products  61 us (11%)
  local copies, waits for them, and re-layouts  46.7 us (8%)
  starting transfers between devices  22.1 us (4%)
  between operations  15.6 us (3%)
  loops' own time  11.2 us (2%)
    reduce_sum x16, other arithmetic, owner_block(): jnp.sum((dedup_map[None, :, :] == wanted[:, None, None]).astype(jnp.float...  181 us
    all_gather x1, waiting for transfers between devices, on_device(): gradient = jnp.sum(lax.all_gather(dense, 'dp'), axis=0)  166 us
    all_to_all x1, waiting for transfers between devices, on_device(): lax.all_to_all(slot_grad, 'table', split_axis=0, concat_axis=0, tiled=True)  51.8 us
    dot_general x16, matrix products, add_source(): jnp.dot(select, grad_block, precision=lax.Precision.HIGHEST, preferred_el...  44.7 us
    dot_general x16, matrix products, owner_block(): jnp.dot(tally.astype(jnp.bfloat16), upstream_grad, preferred_element_type...  16.2 us
    gather x1, local copies, waits for them, and re-layouts, local_targets(): partner_piece = jnp.sum(jnp.where(matches, hot_slices[partner], 0), axis=-1)  14.1 us
  transfers between devices with their start and end apart: 6, of which 4 were waited for; matrix products, arithmetic and copies ran while one was open for 37% of the time, Pallas kernels for 0%

profile of v1, /device:TPU:1, one launch (start us, length us, event | category | flops | bytes accessed | tf_op | source)
XLA Modules:
  0.0 576.3 jit_solution(16917837244179172518)
XLA Ops:
  7.9 3.2 copy.51
  11.1 1.3 copy.52
  12.6 10.8 %gather_fusion = s32[4096,2]{1,0:T(8,128)S(1)} fusion(s32[16,2]{1,0:T(8,128)S(1)} %copy.21, s32[4096]{0:T(1024)S(1)} %broadcast_clamp_fusion.1), kind=kCustom, calls=%fused_computation | custom fusion | bytes 81920 | tf_op jit(solution)/shard_map/gather | solution.py:29
  23.4 14.1 %gather_fusion.1 = s32[4096,2]{1,0:T(8,128)} fusion(s32[16,2]{1,0:T(8,128)S(1)} %copy.21, s32[4096]{0:T(1024)S(1)} %broadcast_clamp_fusion), kind=kCustom, calls=%fused_computation.1 | custom fusion | bytes 81920 | tf_op jit(solution)/shard_map/gather | solution.py:31
  37.5 1.3 fusion.29
  40.5 7.6 %all-to-all-start = ((s32[16,1,256]{2,1,0:T(1,128)}), s32[16,1,256]{2,1,0:T(1,128)S(1)}, u32[]{:S(2)}, u32[]{:S(2)}) async-start(s32[16,1,256]{2,1,0:T(1,128)} %copy.23), calls=%async_computation | async-start | bytes 32768 | tf_op jit(solution)/shard_map/all_to_all | solution.py:97
  48.1 217.9 %while.22 = (s32[]{:T(128)}, f32[16,256,256]{2,1,0:T(8,128)}, s32[1024,32]{0,1:T(8,128)S(1)}, s32[16]{0:T(128)S(1)}, bf16[1024,256]{1,0:T(8,128)(2,1)S(1)}, /*index=5*/s32[]{:T(128)}, s32[1]{0:T(128)}) while((s32[]{:T(128)}, f32[16,256,256]{2,1,0:T(8,128)}, s32[1024,32]{0,1:T(8,128)S(1)}, s32[16]{0:T(128)S(1)}, ...), condition=%wide.region_2.3_spmd.clone, body=%wide.region_0.2_spmd.clone.sunk | while | flops 159121664 | bytes 1968245 | solution.py:94
  49.6 11.3 %convert_reduce_fusion.2 = bf16[256,1024]{1,0:T(8,128)(2,1)S(1)} fusion(s32[1024,32]{0,1:T(8,128)S(1)} %get-tuple-element.201, s32[256]{0:T(256)S(1)} %iota_add_fusion.2), kind=kLoop, calls=%fused_computation.4.clone.1 | loop fusion | flops 24903680 | bytes 656384 | tf_op jit(solution)/shard_map/while/body/eval_jaxpr/reduce_sum | solution.py:86
  60.9 1.0 fusion.39
  63.2 11.3 %convert_reduce_fusion.2 = bf16[256,1024]{1,0:T(8,128)(2,1)S(1)} fusion(s32[1024,32]{0,1:T(8,128)S(1)} %get-tuple-element.201, s32[256]{0:T(256)S(1)} %iota_add_fusion.2), kind=kLoop, calls=%fused_computation.4.clone.1 | loop fusion | flops 24903680 | bytes 656384 | tf_op jit(solution)/shard_map/while/body/eval_jaxpr/reduce_sum | solution.py:86
  74.5 1.0 fusion.39
  76.8 11.3 %convert_reduce_fusion.2 = bf16[256,1024]{1,0:T(8,128)(2,1)S(1)} fusion(s32[1024,32]{0,1:T(8,128)S(1)} %get-tuple-element.201, s32[256]{0:T(256)S(1)} %iota_add_fusion.2), kind=kLoop, calls=%fused_computation.4.clone.1 | loop fusion | flops 24903680 | bytes 656384 | tf_op jit(solution)/shard_map/while/body/eval_jaxpr/reduce_sum | solution.py:86
  88.1 1.0 fusion.39
  90.4 11.3 %convert_reduce_fusion.2 = bf16[256,1024]{1,0:T(8,128)(2,1)S(1)} fusion(s32[1024,32]{0,1:T(8,128)S(1)} %get-tuple-element.201, s32[256]{0:T(256)S(1)} %iota_add_fusion.2), kind=kLoop, calls=%fused_computation.4.clone.1 | loop fusion | flops 24903680 | bytes 656384 | tf_op jit(solution)/shard_map/while/body/eval_jaxpr/reduce_sum | solution.py:86
  104.0 11.3 %convert_reduce_fusion.2 = bf16[256,1024]{1,0:T(8,128)(2,1)S(1)} fusion(s32[1024,32]{0,1:T(8,128)S(1)} %get-tuple-element.201, s32[256]{0:T(256)S(1)} %iota_add_fusion.2), kind=kLoop, calls=%fused_computation.4.clone.1 | loop fusion | flops 24903680 | bytes 656384 | tf_op jit(solution)/shard_map/while/body/eval_jaxpr/reduce_sum | solution.py:86
  115.3 1.0 fusion.39
  117.6 11.3 %convert_reduce_fusion.2 = bf16[256,1024]{1,0:T(8,128)(2,1)S(1)} fusion(s32[1024,32]{0,1:T(8,128)S(1)} %get-tuple-element.201, s32[256]{0:T(256)S(1)} %iota_add_fusion.2), kind=kLoop, calls=%fused_computation.4.clone.1 | loop fusion | flops 24903680 | bytes 656384 | tf_op jit(solution)/shard_map/while/body/eval_jaxpr/reduce_sum | solution.py:86
  129.0 1.0 fusion.39
  131.2 11.3 %convert_reduce_fusion.2 = bf16[256,1024]{1,0:T(8,128)(2,1)S(1)} fusion(s32[1024,32]{0,1:T(8,128)S(1)} %get-tuple-element.201, s32[256]{0:T(256)S(1)} %iota_add_fusion.2), kind=kLoop, calls=%fused_computation.4.clone.1 | loop fusion | flops 24903680 | bytes 656384 | tf_op jit(solution)/shard_map/while/body/eval_jaxpr/reduce_sum | solution.py:86
  142.6 1.0 fusion.39
  144.8 11.3 %convert_reduce_fusion.2 = bf16[256,1024]{1,0:T(8,128)(2,1)S(1)} fusion(s32[1024,32]{0,1:T(8,128)S(1)} %get-tuple-element.201, s32[256]{0:T(256)S(1)} %iota_add_fusion.2), kind=kLoop, calls=%fused_computation.4.clone.1 | loop fusion | flops 24903680 | bytes 656384 | tf_op jit(solution)/shard_map/while/body/eval_jaxpr/reduce_sum | solution.py:86
  156.2 1.0 fusion.39
  158.4 11.3 %convert_reduce_fusion.2 = bf16[256,1024]{1,0:T(8,128)(2,1)S(1)} fusion(s32[1024,32]{0,1:T(8,128)S(1)} %get-tuple-element.201, s32[256]{0:T(256)S(1)} %iota_add_fusion.2), kind=kLoop, calls=%fused_computation.4.clone.1 | loop fusion | flops 24903680 | bytes 656384 | tf_op jit(solution)/shard_map/while/body/eval_jaxpr/reduce_sum | solution.py:86
  169.8 1.0 fusion.39
  172.0 11.3 %convert_reduce_fusion.2 = bf16[256,1024]{1,0:T(8,128)(2,1)S(1)} fusion(s32[1024,32]{0,1:T(8,128)S(1)} %get-tuple-element.201, s32[256]{0:T(256)S(1)} %iota_add_fusion.2), kind=kLoop, calls=%fused_computation.4.clone.1 | loop fusion | flops 24903680 | bytes 656384 | tf_op jit(solution)/shard_map/while/body/eval_jaxpr/reduce_sum | solution.py:86
  183.4 1.0 fusion.39
  185.6 11.3 %convert_reduce_fusion.2 = bf16[256,1024]{1,0:T(8,128)(2,1)S(1)} fusion(s32[1024,32]{0,1:T(8,128)S(1)} %get-tuple-element.201, s32[256]{0:T(256)S(1)} %iota_add_fusion.2), kind=kLoop, calls=%fused_computation.4.clone.1 | loop fusion | flops 24903680 | bytes 656384 | tf_op jit(solution)/shard_map/while/body/eval_jaxpr/reduce_sum | solution.py:86
  197.0 1.0 fusion.39
  199.2 11.3 %convert_reduce_fusion.2 = bf16[256,1024]{1,0:T(8,128)(2,1)S(1)} fusion(s32[1024,32]{0,1:T(8,128)S(1)} %get-tuple-element.201, s32[256]{0:T(256)S(1)} %iota_add_fusion.2), kind=kLoop, calls=%fused_computation.4.clone.1 | loop fusion | flops 24903680 | bytes 656384 | tf_op jit(solution)/shard_map/while/body/eval_jaxpr/reduce_sum | solution.py:86
  210.6 1.0 fusion.39
  212.9 11.3 %convert_reduce_fusion.2 = bf16[256,1024]{1,0:T(8,128)(2,1)S(1)} fusion(s32[1024,32]{0,1:T(8,128)S(1)} %get-tuple-element.201, s32[256]{0:T(256)S(1)} %iota_add_fusion.2), kind=kLoop, calls=%fused_computation.4.clone.1 | loop fusion | flops 24903680 | bytes 656384 | tf_op jit(solution)/shard_map/while/body/eval_jaxpr/reduce_sum | solution.py:86
  226.5 11.3 %convert_reduce_fusion.2 = bf16[256,1024]{1,0:T(8,128)(2,1)S(1)} fusion(s32[1024,32]{0,1:T(8,128)S(1)} %get-tuple-element.201, s32[256]{0:T(256)S(1)} %iota_add_fusion.2), kind=kLoop, calls=%fused_computation.4.clone.1 | loop fusion | flops 24903680 | bytes 656384 | tf_op jit(solution)/shard_map/while/body/eval_jaxpr/reduce_sum | solution.py:86
  237.8 1.0 fusion.39
  240.0 11.3 %convert_reduce_fusion.2 = bf16[256,1024]{1,0:T(8,128)(2,1)S(1)} fusion(s32[1024,32]{0,1:T(8,128)S(1)} %get-tuple-element.201, s32[256]{0:T(256)S(1)} %iota_add_fusion.2), kind=kLoop, calls=%fused_computation.4.clone.1 | loop fusion | flops 24903680 | bytes 656384 | tf_op jit(solution)/shard_map/while/body/eval_jaxpr/reduce_sum | solution.py:86
  253.6 11.3 %convert_reduce_fusion.2 = bf16[256,1024]{1,0:T(8,128)(2,1)S(1)} fusion(s32[1024,32]{0,1:T(8,128)S(1)} %get-tuple-element.201, s32[256]{0:T(256)S(1)} %iota_add_fusion.2), kind=kLoop, calls=%fused_computation.4.clone.1 | loop fusion | flops 24903680 | bytes 656384 | tf_op jit(solution)/shard_map/while/body/eval_jaxpr/reduce_sum | solution.py:86
  265.0 1.1 fusion.39
  266.0 6.7 %all-to-all-start.1 = ((f32[16,256,256]{2,1,0:T(8,128)}), f32[16,256,256]{2,1,0:T(8,128)}, u32[]{:S(2)}, u32[]{:S(2)}) async-start(f32[16,256,256]{2,1,0:T(8,128)} %get-tuple-element.62), calls=%async_computation.1 | async-start | bytes 8388608 | tf_op jit(solution)/shard_map/all_to_all | solution.py:96
  272.8 51.8 %all-to-all-done.1 = f32[16,256,256]{2,1,0:T(8,128)} async-done(((f32[16,256,256]{2,1,0:T(8,128)}), f32[16,256,256]{2,1,0:T(8,128)}, u32[]{:S(2)}, u32[]{:S(2)}) %all-to-all-start.1) | async-done | bytes 4194336 | tf_op jit(solution)/shard_map/all_to_all | solution.py:96
  324.6 45.4 %while.23 = (s32[]{:T(128)}, f32[2048,256]{1,0:T(8,128)S(1)}, s32[16,256]{1,0:T(8,128)S(1)}, f32[16,256,256]{2,1,0:T(8,128)}, s32[]{:T(128)}, /*index=5*/s32[]{:T(128)}) while((s32[]{:T(128)}, f32[2048,256]{1,0:T(8,128)S(1)}, s32[16,256]{1,0:T(8,128)S(1)}, f32[16,256,256]{2,1,0:T(8,128)}, s32[]{:T(128)}, /*index=5*/s32[]{:T(128)}) %tuple.62), condition=%wide.region_6.7_spmd.clone, body=%wide.region_5.6_spmd.clone.sunk | while | flops 1612185600 | bytes 4459615 | solution.py:115
  324.6 2.8 convolution_add_fusion.2
  327.4 2.8 convolution_add_fusion.2
  330.3 2.8 convolution_add_fusion.2
  333.1 2.8 convolution_add_fusion.2
  336.0 2.8 convolution_add_fusion.2
  338.8 2.8 convolution_add_fusion.2
  341.6 2.8 convolution_add_fusion.2
  344.5 2.8 convolution_add_fusion.2
  347.3 2.8 convolution_add_fusion.2
  350.2 2.8 convolution_add_fusion.2
  353.0 2.8 convolution_add_fusion.2
  355.8 2.8 convolution_add_fusion.2
  358.7 2.8 convolution_add_fusion.2
  361.5 2.8 convolution_add_fusion.2
  364.3 2.8 convolution_add_fusion.2
  367.2 2.8 convolution_add_fusion.2
  370.0 1.3 copy-done
  373.5 4.6 collective-permute-start.2
  379.1 3.0 collective-permute-start.1
  382.4 2.1 collective-permute-done
  385.7 1.2 collective-permute-done.1
  388.1 165.6 %all-gather.3.cloned.1.call-done = f32[16384,256]{1,0:T(8,128)} async-done(((f32[2048,256]{1,0:T(8,128)}), f32[16384,256]{1,0:T(8,128)}) %all-gather.3.cloned.1.call-update) | async-done | bytes 16777232 | tf_op jit(solution)/shard_map/all_gather | solution.py:119
  553.7 7.1 %reduce_sum.37 = f32[2048,256]{1,0:T(8,128)S(1)} reduce(f32[8,2048,256]{2,1,0:T(8,128)} %bitcast.104, f32[]{:T(128)} %constant.105.clone.1), dimensions={0}, to_apply=%region_7.8 | reduce | flops 3670016 | bytes 18874372 | tf_op jit(solution)/shard_map/reduce_sum | solution.py:119
  561.2 2.8 psum.7
  564.6 4.8 divide_subtract_fusion
  (101 shorter events, 21.0 us)
Async XLA Ops:
  7.9 3.2 copy-start.4
  11.1 1.3 copy-start.5
  11.1 1.4 copy-start.6
  37.5 1.6 copy-start.2
  37.5 2.3 copy-start.7
  37.5 10.6 %copy-start.1 = (bf16[1024,256]{1,0:T(8,128)(2,1)S(1)}, bf16[1024,256]{1,0:T(8,128)(2,1)}, u32[]{:S(2)}) copy-start(bf16[1024,256]{1,0:T(8,128)(2,1)} %param.16) | copy-start | bytes 1572868
  37.5 10.6 %copy-start.3 = (s32[1024,32]{0,1:T(8,128)S(1)}, s32[1024,32]{0,1:T(8,128)}, u32[]{:S(2)}) copy-start(s32[1024,32]{0,1:T(8,128)} %param.17) | copy-start | bytes 393220
  40.5 225.5 %all-to-all-start = ((s32[16,1,256]{2,1,0:T(1,128)}), s32[16,1,256]{2,1,0:T(1,128)S(1)}, u32[]{:S(2)}, u32[]{:S(2)}) async-start(s32[16,1,256]{2,1,0:T(1,128)} %copy.23), calls=%async_computation | async-start | bytes 32768 | tf_op jit(solution)/shard_map/all_to_all | solution.py:97
  266.0 58.6 %all-to-all-start.1 = ((f32[16,256,256]{2,1,0:T(8,128)}), f32[16,256,256]{2,1,0:T(8,128)}, u32[]{:S(2)}, u32[]{:S(2)}) async-start(f32[16,256,256]{2,1,0:T(8,128)} %get-tuple-element.62), calls=%async_computation.1 | async-start | bytes 8388608 | tf_op jit(solution)/shard_map/all_to_all | solution.py:96
  272.7 281.0 %all-gather.3.cloned.1.call-start = ((), (), s32[]{:S(2)}) async-start(), calls=%async_computation.2 | async-start | bytes 18874368 | tf_op jit(solution)/shard_map/all_gather | solution.py:119
  370.0 1.3 copy-start
  373.5 8.7 %collective-permute-start.2 = (f32[2,64]{1,0:T(2,128)S(1)}, f32[2,64]{1,0:T(2,128)S(1)}, u32[]{:S(2)}, u32[]{:S(2)}) collective-permute-start(f32[2,64]{1,0:T(2,128)S(1)} %pad_maximum_fusion.2), channel_id=1, source_target_pairs={{0,128},{128,0},{16,144},{144,16},{32,160},{160,32},{48,176},{176,... | collective-permute-start | bytes 1544 | tf_op jit(solution)/shard_map/ppermute | solution.py:20
  379.0 5.4 collective-permute-start
  379.1 7.7 %collective-permute-start.1 = (f32[2,64,256]{2,1,0:T(8,128)S(1)}, f32[2,64,256]{2,1,0:T(8,128)S(1)}, u32[]{:S(2)}, u32[]{:S(2)}) collective-permute-start(f32[2,64,256]{2,1,0:T(8,128)S(1)} %pad_maximum_fusion.1), channel_id=1, source_target_pairs={{0,128},{128,0},{16,144},{144,16},{32,160},{160,32},{48,176},{176,... | collective-permute-start | bytes 393224 | tf_op jit(solution)/shard_map/ppermute | solution.py:20
Sparse Core Ops, SparseCore 0:
  371.5 182.1 all-gather.2
